TPU v7x, 128 devices: a whole 4x4x4 slice. The times are simulated.
128 devices in a mesh: wide: 16 (over y, x), narrow: 8 (over z, core).
Axes of the slice: x: 4, y: 4, z: 4, core: 2. Of those that a mesh axis runs over, the one named last changes fastest.
Arguments:
- tokens: bfloat16 [256, 128, 1536], P('wide'), may hold values from -8 to 8
- ln_gain: bfloat16 [1536], replicated, may hold values from 0.3984375 to 1.59375
- gate_weight: bfloat16 [1536, 8960], P(None, 'narrow'), may hold values from -0.15625 to 0.15625
- up_weight: bfloat16 [1536, 8960], P(None, 'narrow'), may hold values from -0.15625 to 0.15625
- down_weight: bfloat16 [8960, 1536], P('narrow'), may hold values from -0.0625 to 0.0625
- out_gain: bfloat16 [1536], replicated, may hold values from 0.25 to 1.75
- shard_ids: int32 [256], P('wide'), may hold values from 0 to 15, as said below
- slab_old: bfloat16 [262144, 1536], P(('wide', 'narrow')), may hold values from -8 to 8
- queries: bfloat16 [16, 64, 1536], P('wide'), may hold values from -12 to 12
- positives: int32 [16, 64], P('wide'), may hold values from 0 to 262399
- owners: int32 [4], replicated, may hold values from 0 to 15
Outputs:
- index_new: bfloat16 [16, 16, 2, 1536], P('wide', 'narrow')
- losses: float32 [4, 64], replicated
Inputs may be any that keep to these rules, and one draw needn't show every extreme that they name: `shard_ids`: among the 16 passages of one index of wide at most 2 have the same shard id; in every draw one shard id is held by exactly 2 passages of every index of wide.
All inputs are finite; a program needn't handle non-finite values.
Results may differ from a plain program's by a relative error of at most 0.0029.
Values may be sent and summed in bfloat16 or wider, within the bound.
No kernel may reach another device: no remote copies, remote signals or barrier semaphores. Data moves between devices by JAX's collectives and lax.ppermute only.
A program may use at most 128 MiB of HBM per device.

v0:
```python
import math
import jax
import jax.numpy as jnp
from jax import lax
from jax.sharding import PartitionSpec as P

EPS = 1e-06


def spread(x, axis, root):
    mine = lax.axis_index(axis) == root
    return lax.psum(jnp.where(mine, x, jnp.zeros_like(x)), axis)


def rms_scale(values):
    return lax.rsqrt(jnp.mean(values * values, axis=-1, keepdims=True) + EPS)


def local(
    tokens,
    ln_gain,
    gate_weight,
    up_weight,
    down_weight,
    out_gain,
    shard_ids,
    slab_old,
    queries,
    positives,
    owners,
):
    passages, seq_len, width = tokens.shape
    narrow_count = lax.axis_size("narrow")
    wide_count = lax.axis_size("wide")
    narrow_rank = lax.axis_index("narrow")
    wide_rank = lax.axis_index("wide")
    piece_width = width // narrow_count
    capacity = 2 * passages // wide_count
    values = tokens.astype(jnp.float32)
    normed = (values * rms_scale(values) * ln_gain.astype(jnp.float32)).astype(jnp.bfloat16)
    normed = normed.reshape(passages * seq_len, width)
    gate = jnp.dot(normed, gate_weight, preferred_element_type=jnp.float32)
    upward = jnp.dot(normed, up_weight, preferred_element_type=jnp.float32)
    hidden = (jax.nn.silu(gate) * upward).astype(jnp.bfloat16)
    partial_value = jnp.dot(hidden, down_weight, preferred_element_type=jnp.float32)
    pooled_part = jnp.mean(partial_value.reshape(passages, seq_len, width), axis=1)
    token_mean = jnp.mean(values, axis=1)
    offset = narrow_rank * piece_width
    pooled = lax.psum(pooled_part, "narrow") + token_mean
    norm_scale = rms_scale(pooled)
    own_piece = lax.dynamic_slice_in_dim(pooled, offset, piece_width, 1)
    gain_piece = lax.dynamic_slice_in_dim(out_gain.astype(jnp.float32), offset, piece_width, 0)
    embedding = (own_piece * norm_scale * gain_piece).astype(jnp.bfloat16)
    positions = jnp.arange(passages, dtype=jnp.int32)
    earlier = positions[:, None] > positions[None, :]
    same = shard_ids[:, None] == shard_ids[None, :]
    rank = jnp.sum((earlier & same).astype(jnp.int32), axis=1)
    slots = shard_ids * capacity + rank
    dispatch = slots[None, :] == jnp.arange(wide_count * capacity, dtype=jnp.int32)[:, None]
    outgoing = jnp.dot(dispatch.astype(jnp.bfloat16), embedding, preferred_element_type=jnp.float32)
    outgoing = outgoing.astype(jnp.bfloat16).reshape(wide_count, capacity, piece_width)
    numbers = wide_rank * passages + positions
    slot_numbers = jnp.sum(jnp.where(dispatch, numbers[None, :] + 1, 0), axis=1) - 1
    slot_numbers = slot_numbers.reshape(wide_count, capacity, 1)
    arrived, arrived_numbers = (
        lax.all_to_all(
            lax.all_to_all(outgoing, "wide", split_axis=0, concat_axis=0, tiled=True),
            "narrow",
            split_axis=0,
            concat_axis=2,
            tiled=True,
        ),
        lax.all_to_all(
            lax.all_to_all(slot_numbers, "wide", split_axis=0, concat_axis=0, tiled=True),
            "narrow",
            split_axis=0,
            concat_axis=2,
            tiled=True,
        ),
    )
    old_total = slab_old.shape[0] * wide_count * narrow_count
    new_rows = arrived.reshape(-1, width)
    new_numbers = arrived_numbers[:, :, 0].reshape(-1)
    valid = (new_numbers >= 0)[None, :]
    new_global = old_total + new_numbers
    device_linear = wide_rank * narrow_count + narrow_rank
    old_global = device_linear * slab_old.shape[0] + jnp.arange(slab_old.shape[0], dtype=jnp.int32)
    scale = 1.0 / math.sqrt(width)
    contract = (((1,), (1,)), ((), ()))
    block_size = queries.shape[1]
    step_count = owners.shape[0]

    def score_rows(block, positive):
        old_scores = (
            lax.dot_general(block, slab_old, contract, preferred_element_type=jnp.float32) * scale
        )
        new_scores = (
            lax.dot_general(block, new_rows, contract, preferred_element_type=jnp.float32) * scale
        )
        masked = jnp.where(valid, new_scores, -jnp.inf)
        local_max = jnp.maximum(jnp.max(old_scores, axis=1), jnp.max(masked, axis=1))
        hit_old = old_global[None, :] == positive[:, None]
        hit_new = valid & (new_global[None, :] == positive[:, None])
        local_positive = jnp.sum(jnp.where(hit_old, old_scores, 0.0), axis=1) + jnp.sum(
            jnp.where(hit_new, new_scores, 0.0), axis=1
        )
        largest = lax.pmax(local_max, ("wide", "narrow"))
        local_total = jnp.sum(jnp.exp(old_scores - largest[:, None]), axis=1)
        local_total = local_total + jnp.sum(
            jnp.where(valid, jnp.exp(new_scores - largest[:, None]), 0.0), axis=1
        )
        total, picked = lax.psum((local_total, local_positive), ("wide", "narrow"))
        return largest + jnp.log(total) - picked

    def step_body(step, losses):
        owner = owners[step]
        block, positive = (spread(queries[0], "wide", owner), spread(positives[0], "wide", owner))
        loss = score_rows(block, positive)
        return lax.dynamic_update_slice_in_dim(losses, loss[None, :], step, 0)

    start_losses = jnp.zeros((step_count, block_size), jnp.float32)
    losses = lax.fori_loop(0, step_count, step_body, start_losses)
    return (arrived[None], losses)


def solution(mesh):
    return jax.shard_map(
        local,
        mesh=mesh,
        in_specs=(
            P("wide", None, None),
            P(),
            P(None, "narrow"),
            P(None, "narrow"),
            P("narrow", None),
            P(),
            P("wide"),
            P(("wide", "narrow"), None),
            P("wide", None, None),
            P("wide", None),
            P(),
        ),
        out_specs=(P("wide", "narrow", None, None), P()),
        check_vma=False,
    )
```

profile of v0, /device:TPU:1, one launch (start us, length us, event | category | flops | bytes accessed | tf_op | source)
XLA Modules:
  0.0 1026.5 jit_solution(8330299875181176620)
XLA Ops:
  8.1 4.9 convert_reduce_fusion
  17.2 9.7 fusion.16
  26.9 22.3 %bitcast_reduce_fusion = f32[16,1536]{1,0:T(8,128)} fusion(bf16[1120,1536]{1,0:T(8,128)(2,1)} %param.17, bf16[2048,1536]{1,0:T(8,128)(2,1)} %bitcast.51, bf16[1536,1120]{0,1:T(8,128)(2,1)} %param.16, f32[2048,1120]{0,1:T(8,128)} %fusion.16), kind=kOutput, calls=%fused_computation.19 | convolution fusion | flops 14109745152 | bytes 22446080 | tf_op jit(solution)/shard_map/dot_general | solution.py:45
  51.8 7.6 all-to-all-start.2
  60.8 4.9 all-to-all-done.2
  65.7 7.6 all-to-all-start.3
  73.2 4.6 all-to-all-done.3
  78.1 32.4 %all-reduce.6.cloned.1.call-done = f32[16,1536]{1,0:T(8,128)} async-done(((f32[16,1536]{1,0:T(8,128)}), f32[16,1536]{1,0:T(8,128)}) %all-reduce.6.cloned.1.call-update) | async-done | bytes 98320 | tf_op jit(solution)/shard_map/psum | solution.py:49
  113.1 6.6 all-to-all-start
  119.8 6.3 all-to-all-done
  126.2 7.2 all-to-all-start.1
  138.8 881.1 %while.14 = (s32[]{:T(128)}, f32[4,64]{1,0:T(4,128)}, s32[4]{0:T(128)}, bf16[1,64,1536]{2,1,0:T(8,128)(2,1)}, bf16[2048,1536]{1,0:T(8,128)(2,1)}, /*index=5*/pre...) while((s32[]{:T(128)}, f32[4,64]{1,0:T(4,128)}, ...), condition=%wide.region_19.20_spmd.clone, body=%wide.region_7.19_spmd.clone.sunk | while | flops 404558592 | bytes 10132520 | solution.py:122
  141.6 9.3 psum.59
  150.9 69.7 %all-reduce.8.cloned.1.call-done = bf16[64,1536]{1,0:T(8,128)(2,1)} async-done(((bf16[64,1536]{1,0:T(8,128)(2,1)}), bf16[64,1536]{1,0:T(8,128)(2,1)}) %all-reduce.8.cloned.1.call-update) | async-done | bytes 196624 | tf_op jit(solution)/shard_map/while/body/eval_jaxpr/psum | solution.py:12
  220.6 5.8 fusion.36
  226.6 66.3 %pmax.13 = f32[64]{0:T(128)S(1)} all-reduce(f32[64]{0:T(128)S(1)} %max.11), channel_id=1, replica_groups=mesh['wide'=16,'narrow'=8] {'wide','narrow'}, use_global_device_ids=true, to_apply=%region_11.11 | all-reduce | flops 64 | bytes 512 | tf_op jit(solution)/shard_map/while/body/eval_jaxpr/pmax | solution.py:107
  294.4 62.5 %all-reduce.2 = (f32[64]{0:T(128)S(1)}, f32[64]{0:T(128)S(1)}) all-reduce(f32[64]{0:T(128)S(1)} %add.187, f32[64]{0:T(128)S(1)} %add.188), channel_id=1, replica_groups=mesh['wide'=16,'narrow'=8] {'wide','narrow'}, use_global_device_ids=true, to_apply=%region_18.18 | all-reduce | flops 128 | bytes 1024 | tf_op jit(solution)/shard_map/while/body/eval_jaxpr/psum | solution.py:112
  361.0 10.9 %psum.59 = s32[64]{0:T(128)S(1)} all-reduce(s32[64]{0:T(128)S(1)} %fusion.37), channel_id=1, replica_groups=mesh['wide'=16,'narrow'=8] {'wide'}, use_global_device_ids=true, to_apply=%region_15.15 | all-reduce | flops 64 | bytes 512 | tf_op jit(solution)/shard_map/while/body/eval_jaxpr/psum | solution.py:12
  371.8 69.6 %all-reduce.8.cloned.1.call-done = bf16[64,1536]{1,0:T(8,128)(2,1)} async-done(((bf16[64,1536]{1,0:T(8,128)(2,1)}), bf16[64,1536]{1,0:T(8,128)(2,1)}) %all-reduce.8.cloned.1.call-update) | async-done | bytes 196624 | tf_op jit(solution)/shard_map/while/body/eval_jaxpr/psum | solution.py:12
  441.4 5.8 fusion.36
  447.4 66.4 %pmax.13 = f32[64]{0:T(128)S(1)} all-reduce(f32[64]{0:T(128)S(1)} %max.11), channel_id=1, replica_groups=mesh['wide'=16,'narrow'=8] {'wide','narrow'}, use_global_device_ids=true, to_apply=%region_11.11 | all-reduce | flops 64 | bytes 512 | tf_op jit(solution)/shard_map/while/body/eval_jaxpr/pmax | solution.py:107
  515.2 62.5 %all-reduce.2 = (f32[64]{0:T(128)S(1)}, f32[64]{0:T(128)S(1)}) all-reduce(f32[64]{0:T(128)S(1)} %add.187, f32[64]{0:T(128)S(1)} %add.188), channel_id=1, replica_groups=mesh['wide'=16,'narrow'=8] {'wide','narrow'}, use_global_device_ids=true, to_apply=%region_18.18 | all-reduce | flops 128 | bytes 1024 | tf_op jit(solution)/shard_map/while/body/eval_jaxpr/psum | solution.py:112
  583.3 9.0 psum.59
  592.3 69.5 %all-reduce.8.cloned.1.call-done = bf16[64,1536]{1,0:T(8,128)(2,1)} async-done(((bf16[64,1536]{1,0:T(8,128)(2,1)}), bf16[64,1536]{1,0:T(8,128)(2,1)}) %all-reduce.8.cloned.1.call-update) | async-done | bytes 196624 | tf_op jit(solution)/shard_map/while/body/eval_jaxpr/psum | solution.py:12
  661.9 5.8 fusion.36
  667.9 66.3 %pmax.13 = f32[64]{0:T(128)S(1)} all-reduce(f32[64]{0:T(128)S(1)} %max.11), channel_id=1, replica_groups=mesh['wide'=16,'narrow'=8] {'wide','narrow'}, use_global_device_ids=true, to_apply=%region_11.11 | all-reduce | flops 64 | bytes 512 | tf_op jit(solution)/shard_map/while/body/eval_jaxpr/pmax | solution.py:107
  735.7 62.5 %all-reduce.2 = (f32[64]{0:T(128)S(1)}, f32[64]{0:T(128)S(1)}) all-reduce(f32[64]{0:T(128)S(1)} %add.187, f32[64]{0:T(128)S(1)} %add.188), channel_id=1, replica_groups=mesh['wide'=16,'narrow'=8] {'wide','narrow'}, use_global_device_ids=true, to_apply=%region_18.18 | all-reduce | flops 128 | bytes 1024 | tf_op jit(solution)/shard_map/while/body/eval_jaxpr/psum | solution.py:112
  802.2 11.2 %psum.59 = s32[64]{0:T(128)S(1)} all-reduce(s32[64]{0:T(128)S(1)} %fusion.37), channel_id=1, replica_groups=mesh['wide'=16,'narrow'=8] {'wide'}, use_global_device_ids=true, to_apply=%region_15.15 | all-reduce | flops 64 | bytes 512 | tf_op jit(solution)/shard_map/while/body/eval_jaxpr/psum | solution.py:12
  813.4 68.9 %all-reduce.8.cloned.1.call-done = bf16[64,1536]{1,0:T(8,128)(2,1)} async-done(((bf16[64,1536]{1,0:T(8,128)(2,1)}), bf16[64,1536]{1,0:T(8,128)(2,1)}) %all-reduce.8.cloned.1.call-update) | async-done | bytes 196624 | tf_op jit(solution)/shard_map/while/body/eval_jaxpr/psum | solution.py:12
  882.4 5.8 fusion.36
  888.4 66.3 %pmax.13 = f32[64]{0:T(128)S(1)} all-reduce(f32[64]{0:T(128)S(1)} %max.11), channel_id=1, replica_groups=mesh['wide'=16,'narrow'=8] {'wide','narrow'}, use_global_device_ids=true, to_apply=%region_11.11 | all-reduce | flops 64 | bytes 512 | tf_op jit(solution)/shard_map/while/body/eval_jaxpr/pmax | solution.py:107
  956.2 62.5 %all-reduce.2 = (f32[64]{0:T(128)S(1)}, f32[64]{0:T(128)S(1)}) all-reduce(f32[64]{0:T(128)S(1)} %add.187, f32[64]{0:T(128)S(1)} %add.188), channel_id=1, replica_groups=mesh['wide'=16,'narrow'=8] {'wide','narrow'}, use_global_device_ids=true, to_apply=%region_18.18 | all-reduce | flops 128 | bytes 1024 | tf_op jit(solution)/shard_map/while/body/eval_jaxpr/psum | solution.py:112
  (102 shorter events, 38.8 us)
Async XLA Ops:
  7.2 10.1 copy-start
  7.2 103.3 %all-reduce.6.cloned.1.call-start = ((), (), s32[]{:S(2)}) async-start(), calls=%async_computation.4 | async-start | bytes 196608 | tf_op jit(solution)/shard_map/psum | solution.py:49
  7.2 5.8 copy-start.1
  14.5 2.7 copy-start.2
  26.9 23.8 %copy-start.4 = (s32[16]{0:T(128)S(1)}, s32[16]{0:T(128)}, u32[]{:S(2)}) copy-start(s32[16]{0:T(128)} %param.19) | copy-start | bytes 196
  50.9 26.9 %copy-start.5 = (s32[16]{0:T(128)}, s32[16]{0:T(128)S(1)}, u32[]{:S(2)}) copy-start(s32[16]{0:T(128)S(1)} %multiply_add_fusion.1) | copy-start | bytes 196
  51.8 13.9 %all-to-all-start.2 = ((s32[16,2,1]{1,2,0:T(1,128)}), s32[16,2,1]{1,2,0:T(1,128)}, u32[]{:S(2)}, u32[]{:S(2)}) async-start(s32[16,2,1]{1,2,0:T(1,128)} %bitcast.4), calls=%async_computation.2 | async-start | bytes 16384 | tf_op jit(solution)/shard_map/all_to_all | solution.py:74
  65.7 12.2 %all-to-all-start.3 = ((s32[16,2,1]{1,2,0:T(1,128)}), s32[16,2,1]{1,2,0:T(1,128)S(1)}, u32[]{:S(2)}, u32[]{:S(2)}) async-start(s32[16,2,1]{1,2,0:T(1,128)} %all-to-all-done.2), calls=%async_computation.3 | async-start | bytes 16384 | tf_op jit(solution)/shard_map/all_to_all | solution.py:73
  113.1 13.1 %all-to-all-start = ((bf16[16,2,192]{2,1,0:T(2,128)(2,1)}), bf16[16,2,192]{2,1,0:T(2,128)(2,1)}, u32[]{:S(2)}, u32[]{:S(2)}) async-start(bf16[16,2,192]{2,1,0:T(2,128)(2,1)} %reshape.84), calls=%async_computation | async-start | bytes 32768 | tf_op jit(solution)/shard_map/all_to_all | solution.py:67
  126.2 11.9 %all-to-all-start.1 = ((bf16[16,2,192]{2,1,0:T(2,128)(2,1)}), bf16[16,2,192]{2,1,0:T(2,128)(2,1)S(1)}, u32[]{:S(2)}, u32[]{:S(2)}) async-start(bf16[16,2,192]{2,1,0:T(2,128)(2,1)} %all-to-all-done), calls=%async_computation.1 | async-start | bytes 32768 | tf_op jit(solution)/shard_map/all_to_all | solution.py:66
  138.8 81.8 %all-reduce.8.cloned.1.call-start = ((), (), s32[]{:S(2)}) async-start(), calls=%async_computation.5 | async-start | bytes 393216 | tf_op jit(solution)/shard_map/while/body/eval_jaxpr/psum | solution.py:12
  220.6 5.8 copy-start.3
  358.2 83.2 %all-reduce.8.cloned.1.call-start = ((), (), s32[]{:S(2)}) async-start(), calls=%async_computation.5 | async-start | bytes 393216 | tf_op jit(solution)/shard_map/while/body/eval_jaxpr/psum | solution.py:12
  441.4 5.8 copy-start.3
  579.0 82.9 %all-reduce.8.cloned.1.call-start = ((), (), s32[]{:S(2)}) async-start(), calls=%async_computation.5 | async-start | bytes 393216 | tf_op jit(solution)/shard_map/while/body/eval_jaxpr/psum | solution.py:12
  661.9 5.8 copy-start.3
  799.5 82.9 %all-reduce.8.cloned.1.call-start = ((), (), s32[]{:S(2)}) async-start(), calls=%async_computation.5 | async-start | bytes 393216 | tf_op jit(solution)/shard_map/while/body/eval_jaxpr/psum | solution.py:12
  882.4 5.8 copy-start.3
Sparse Core Ops, SparseCore 0:
  50.9 59.5 all-reduce.5
  142.8 77.7 all-reduce.7
  362.2 79.1 all-reduce.7
  582.8 79.0 all-reduce.7
  803.2 79.1 all-reduce.7
where the time goes:
time: 1030 us
  blocking collectives  556 us (54%)
  waiting for transfers between devices  330 us (32%)
  matrix products  56.9 us (6%)
  starting transfers between devices  29 us (3%)
  other arithmetic  22 us (2%)
  local copies, waits for them, and re-layouts  15.6 us (2%)
  between operations  13.8 us (1%)
    psum x4, waiting for transfers between devices, spread(): return lax.psum(jnp.where(mine, x, jnp.zeros_like(x)), axis)  278 us
    pmax x4, blocking collectives, score_rows(): largest = lax.pmax(local_max, ('wide', 'narrow'))  265 us
    psum x4, blocking collectives, score_rows(): total, picked = lax.psum((local_total, local_positive), ('wide', 'narrow'))  250 us
    psum x4, blocking collectives, spread(): return lax.psum(jnp.where(mine, x, jnp.zeros_like(x)), axis)  40.4 us
    psum x1, waiting for transfers between devices, local(): pooled = lax.psum(pooled_part, 'narrow') + token_mean  32.4 us
    dot_general x4, matrix products, score_rows(): lax.dot_general(block, slab_old, contract, preferred_element_type=jnp.flo...  23.3 us
    dot_general x1, matrix products, local(): jnp.dot(hidden, down_weight, preferred_element_type=jnp.float32)  22.3 us
  transfers between devices with their start and end apart: 9, of which 9 were waited for; matrix products, arithmetic and copies ran while one was open for 0% of the time, Pallas kernels for 0%

commit v1 on v0

--- a/solution.py
+++ b/solution.py
@@ -7,9 +7,15 @@
 EPS = 1e-06
 
 
+def add_all(value, mesh_axis):
+    terms = lax.all_gather(value, mesh_axis, axis=0, tiled=False)
+    result = terms.sum(axis=0)
+    return result
+
+
 def spread(x, axis, root):
     mine = lax.axis_index(axis) == root
-    return lax.psum(jnp.where(mine, x, jnp.zeros_like(x)), axis)
+    return add_all(jnp.where(mine, x, jnp.zeros_like(x)), axis)
 
 
 def rms_scale(values):

time: 1030 us -> 894 us (0.87)
  waiting for transfers between devices: 330 us -> 168 us
  blocking collectives: 556 us -> 572 us
  other arithmetic: 22 us -> 34.4 us
    psum x4 -> x0, waiting for transfers between devices: 278 us -> none  [spread(): return lax.psum(jnp.where(mine, x, jnp.zeros_like(x)), axis)]
    all_gather x0 -> x4, waiting for transfers between devices: none -> 115 us  [add_all(): terms = lax.all_gather(value, mesh_axis, axis=0, tiled=False)]
    all_gather x0 -> x4, blocking collectives: none -> 58.2 us  [add_all(): terms = lax.all_gather(value, mesh_axis, axis=0, tiled=False)]
    psum x4 -> x0, blocking collectives: 40.4 us -> none  [spread(): return lax.psum(jnp.where(mine, x, jnp.zeros_like(x)), axis)]
    reduce_sum x0 -> x8, other arithmetic: none -> 12.4 us  [add_all(): result = terms.sum(axis=0)]
where the time goes in v1:
time: 894 us; the launch traced here: 892 us
  blocking collectives  572 us (64%)
  waiting for transfers between devices  168 us (19%)
  matrix products  56.9 us (6%)
  other arithmetic  34.4 us (4%)
  starting transfers between devices  29 us (3%)
  local copies, waits for them, and re-layouts  15.6 us (2%)
  between operations  13.8 us (2%)
    pmax x4, blocking collectives, score_rows(): largest = lax.pmax(local_max, ('wide', 'narrow'))  259 us
    psum x4, blocking collectives, score_rows(): total, picked = lax.psum((local_total, local_positive), ('wide', 'narrow'))  254 us
    all_gather x4, waiting for transfers between devices, add_all(): terms = lax.all_gather(value, mesh_axis, axis=0, tiled=False)  115 us
    all_gather x4, blocking collectives, add_all(): terms = lax.all_gather(value, mesh_axis, axis=0, tiled=False)  58.2 us
    psum x1, waiting for transfers between devices, local(): pooled = lax.psum(pooled_part, 'narrow') + token_mean  32.4 us
    dot_general x4, matrix products, score_rows(): lax.dot_general(block, slab_old, contract, preferred_element_type=jnp.flo...  23.3 us
    dot_general x1, matrix products, local(): jnp.dot(hidden, down_weight, preferred_element_type=jnp.float32)  22.3 us
  transfers between devices with their start and end apart: 9, of which 9 were waited for; matrix products, arithmetic and copies ran while one was open for 0% of the time, Pallas kernels for 0%

profile of v1, /device:TPU:1, one launch (start us, length us, event | category | flops | bytes accessed | tf_op | source)
XLA Modules:
  0.0 892.1 jit_solution(16426637352766159025)
XLA Ops:
  8.1 4.9 convert_reduce_fusion
  17.2 9.7 %fusion.16 = f32[2048,1120]{0,1:T(8,128)} fusion(bf16[2048,1536]{1,0:T(8,128)(2,1)S(1)} %bitcast.46, bf16[1536,1120]{0,1:T(8,128)(2,1)S(1)} %copy-done), kind=kOutput, calls=%fused_computation.49 | convolution fusion | flops 7046430720 | bytes 18907136 | tf_op jit(solution)/shard_map/dot_general | solution.py:48
  26.9 22.3 %bitcast_reduce_fusion = f32[16,1536]{1,0:T(8,128)} fusion(bf16[1120,1536]{1,0:T(8,128)(2,1)} %param.17, bf16[2048,1536]{1,0:T(8,128)(2,1)} %bitcast.47, bf16[1536,1120]{0,1:T(8,128)(2,1)} %param.16, f32[2048,1120]{0,1:T(8,128)} %fusion.16), kind=kOutput, calls=%fused_computation.19 | convolution fusion | flops 14109745152 | bytes 22446080 | tf_op jit(solution)/shard_map/dot_general | solution.py:51
  51.8 7.6 all-to-all-start.2
  60.8 4.9 all-to-all-done.2
  65.7 7.6 all-to-all-start.3
  73.2 4.6 all-to-all-done.3
  78.1 32.4 %all-reduce.5.cloned.1.call-done = f32[16,1536]{1,0:T(8,128)} async-done(((f32[16,1536]{1,0:T(8,128)}), f32[16,1536]{1,0:T(8,128)}) %all-reduce.5.cloned.1.call-update) | async-done | bytes 98320 | tf_op jit(solution)/shard_map/psum | solution.py:55
  113.1 6.6 all-to-all-start
  119.8 6.3 all-to-all-done
  126.2 7.2 all-to-all-start.1
  138.8 746.8 %while.16 = (s32[]{:T(128)}, f32[4,64]{1,0:T(4,128)}, s32[4]{0:T(128)}, bf16[1,64,1536]{2,1,0:T(8,128)(2,1)}, bf16[2048,1536]{1,0:T(8,128)(2,1)}, /*index=5*/pre...) while((s32[]{:T(128)}, f32[4,64]{1,0:T(4,128)}, ...), condition=%wide.region_19.20_spmd.clone, body=%wide.region_7.19_spmd.clone.sunk | while | flops 405935744 | bytes 22330420 | solution.py:128
  141.6 14.7 %all-gather.3 = s32[16,1,64]{2,1,0:T(1,128)S(1)} all-gather(s32[1,1,64]{2,1,0:T(1,128)S(1)} %fusion.37), channel_id=1, replica_groups=mesh['wide'=16,'narrow'=8] {'wide'}, dimensions={0}, use_global_device_ids=true | all-gather | bytes 4352 | tf_op jit(solution)/shard_map/while/body/eval_jaxpr/all_gather | solution.py:11
  156.4 28.1 %all-gather.6.cloned.1.call-done = bf16[16,64,1536]{2,1,0:T(8,128)(2,1)} async-done(((bf16[1,64,1536]{2,1,0:T(8,128)(2,1)}), bf16[16,64,1536]{2,1,0:T(8,128)(2,1)}) %all-gather.6.cloned.1.call-update) | async-done | bytes 3145744 | tf_op jit(solution)/shard_map/while/body/eval_jaxpr/all_gather | solution.py:11
  187.6 5.8 fusion.36
  193.6 64.8 %pmax.16 = f32[64]{0:T(128)S(1)} all-reduce(f32[64]{0:T(128)S(1)} %max.14), channel_id=1, replica_groups=mesh['wide'=16,'narrow'=8] {'wide','narrow'}, use_global_device_ids=true, to_apply=%region_11.11 | all-reduce | flops 64 | bytes 512 | tf_op jit(solution)/shard_map/while/body/eval_jaxpr/pmax | solution.py:113
  259.9 63.5 %all-reduce.2 = (f32[64]{0:T(128)S(1)}, f32[64]{0:T(128)S(1)}) all-reduce(f32[64]{0:T(128)S(1)} %add.199, f32[64]{0:T(128)S(1)} %add.200), channel_id=1, replica_groups=mesh['wide'=16,'narrow'=8] {'wide','narrow'}, use_global_device_ids=true, to_apply=%region_18.18 | all-reduce | flops 128 | bytes 1024 | tf_op jit(solution)/shard_map/while/body/eval_jaxpr/psum | solution.py:118
  327.4 14.9 %all-gather.3 = s32[16,1,64]{2,1,0:T(1,128)S(1)} all-gather(s32[1,1,64]{2,1,0:T(1,128)S(1)} %fusion.37), channel_id=1, replica_groups=mesh['wide'=16,'narrow'=8] {'wide'}, dimensions={0}, use_global_device_ids=true | all-gather | bytes 4352 | tf_op jit(solution)/shard_map/while/body/eval_jaxpr/all_gather | solution.py:11
  342.4 29.4 %all-gather.6.cloned.1.call-done = bf16[16,64,1536]{2,1,0:T(8,128)(2,1)} async-done(((bf16[1,64,1536]{2,1,0:T(8,128)(2,1)}), bf16[16,64,1536]{2,1,0:T(8,128)(2,1)}) %all-gather.6.cloned.1.call-update) | async-done | bytes 3145744 | tf_op jit(solution)/shard_map/while/body/eval_jaxpr/all_gather | solution.py:11
  374.8 5.8 fusion.36
  380.8 64.8 %pmax.16 = f32[64]{0:T(128)S(1)} all-reduce(f32[64]{0:T(128)S(1)} %max.14), channel_id=1, replica_groups=mesh['wide'=16,'narrow'=8] {'wide','narrow'}, use_global_device_ids=true, to_apply=%region_11.11 | all-reduce | flops 64 | bytes 512 | tf_op jit(solution)/shard_map/while/body/eval_jaxpr/pmax | solution.py:113
  447.1 63.5 %all-reduce.2 = (f32[64]{0:T(128)S(1)}, f32[64]{0:T(128)S(1)}) all-reduce(f32[64]{0:T(128)S(1)} %add.199, f32[64]{0:T(128)S(1)} %add.200), channel_id=1, replica_groups=mesh['wide'=16,'narrow'=8] {'wide','narrow'}, use_global_device_ids=true, to_apply=%region_18.18 | all-reduce | flops 128 | bytes 1024 | tf_op jit(solution)/shard_map/while/body/eval_jaxpr/psum | solution.py:118
  516.2 13.4 %all-gather.3 = s32[16,1,64]{2,1,0:T(1,128)S(1)} all-gather(s32[1,1,64]{2,1,0:T(1,128)S(1)} %fusion.37), channel_id=1, replica_groups=mesh['wide'=16,'narrow'=8] {'wide'}, dimensions={0}, use_global_device_ids=true | all-gather | bytes 4352 | tf_op jit(solution)/shard_map/while/body/eval_jaxpr/all_gather | solution.py:11
  529.7 28.5 %all-gather.6.cloned.1.call-done = bf16[16,64,1536]{2,1,0:T(8,128)(2,1)} async-done(((bf16[1,64,1536]{2,1,0:T(8,128)(2,1)}), bf16[16,64,1536]{2,1,0:T(8,128)(2,1)}) %all-gather.6.cloned.1.call-update) | async-done | bytes 3145744 | tf_op jit(solution)/shard_map/while/body/eval_jaxpr/all_gather | solution.py:11
  561.3 5.8 fusion.36
  567.3 64.8 %pmax.16 = f32[64]{0:T(128)S(1)} all-reduce(f32[64]{0:T(128)S(1)} %max.14), channel_id=1, replica_groups=mesh['wide'=16,'narrow'=8] {'wide','narrow'}, use_global_device_ids=true, to_apply=%region_11.11 | all-reduce | flops 64 | bytes 512 | tf_op jit(solution)/shard_map/while/body/eval_jaxpr/pmax | solution.py:113
  633.6 63.5 %all-reduce.2 = (f32[64]{0:T(128)S(1)}, f32[64]{0:T(128)S(1)}) all-reduce(f32[64]{0:T(128)S(1)} %add.199, f32[64]{0:T(128)S(1)} %add.200), channel_id=1, replica_groups=mesh['wide'=16,'narrow'=8] {'wide','narrow'}, use_global_device_ids=true, to_apply=%region_18.18 | all-reduce | flops 128 | bytes 1024 | tf_op jit(solution)/shard_map/while/body/eval_jaxpr/psum | solution.py:118
  701.1 15.2 %all-gather.3 = s32[16,1,64]{2,1,0:T(1,128)S(1)} all-gather(s32[1,1,64]{2,1,0:T(1,128)S(1)} %fusion.37), channel_id=1, replica_groups=mesh['wide'=16,'narrow'=8] {'wide'}, dimensions={0}, use_global_device_ids=true | all-gather | bytes 4352 | tf_op jit(solution)/shard_map/while/body/eval_jaxpr/all_gather | solution.py:11
  716.4 29.0 %all-gather.6.cloned.1.call-done = bf16[16,64,1536]{2,1,0:T(8,128)(2,1)} async-done(((bf16[1,64,1536]{2,1,0:T(8,128)(2,1)}), bf16[16,64,1536]{2,1,0:T(8,128)(2,1)}) %all-gather.6.cloned.1.call-update) | async-done | bytes 3145744 | tf_op jit(solution)/shard_map/while/body/eval_jaxpr/all_gather | solution.py:11
  748.5 5.8 fusion.36
  754.5 64.8 %pmax.16 = f32[64]{0:T(128)S(1)} all-reduce(f32[64]{0:T(128)S(1)} %max.14), channel_id=1, replica_groups=mesh['wide'=16,'narrow'=8] {'wide','narrow'}, use_global_device_ids=true, to_apply=%region_11.11 | all-reduce | flops 64 | bytes 512 | tf_op jit(solution)/shard_map/while/body/eval_jaxpr/pmax | solution.py:113
  820.8 63.5 %all-reduce.2 = (f32[64]{0:T(128)S(1)}, f32[64]{0:T(128)S(1)}) all-reduce(f32[64]{0:T(128)S(1)} %add.199, f32[64]{0:T(128)S(1)} %add.200), channel_id=1, replica_groups=mesh['wide'=16,'narrow'=8] {'wide','narrow'}, use_global_device_ids=true, to_apply=%region_18.18 | all-reduce | flops 128 | bytes 1024 | tf_op jit(solution)/shard_map/while/body/eval_jaxpr/psum | solution.py:118
  (110 shorter events, 51.2 us)
Async XLA Ops:
  7.2 10.1 %copy-start = (bf16[1536,1120]{0,1:T(8,128)(2,1)S(1)}, bf16[1536,1120]{0,1:T(8,128)(2,1)}, u32[]{:S(2)}) copy-start(bf16[1536,1120]{0,1:T(8,128)(2,1)} %param.15) | copy-start | bytes 10321924
  7.2 103.3 %all-reduce.5.cloned.1.call-start = ((), (), s32[]{:S(2)}) async-start(), calls=%async_computation.4 | async-start | bytes 196608 | tf_op jit(solution)/shard_map/psum | solution.py:55
  7.2 5.8 copy-start.1
  14.5 2.7 copy-start.3
  26.9 23.8 %copy-start.4 = (s32[16]{0:T(128)S(1)}, s32[16]{0:T(128)}, u32[]{:S(2)}) copy-start(s32[16]{0:T(128)} %param.19) | copy-start | bytes 196
  50.9 26.9 %copy-start.5 = (s32[16]{0:T(128)}, s32[16]{0:T(128)S(1)}, u32[]{:S(2)}) copy-start(s32[16]{0:T(128)S(1)} %multiply_add_fusion.1) | copy-start | bytes 196
  51.8 13.9 %all-to-all-start.2 = ((s32[16,2,1]{1,2,0:T(1,128)}), s32[16,2,1]{1,2,0:T(1,128)}, u32[]{:S(2)}, u32[]{:S(2)}) async-start(s32[16,2,1]{1,2,0:T(1,128)} %bitcast.4), calls=%async_computation.2 | async-start | bytes 16384 | tf_op jit(solution)/shard_map/all_to_all | solution.py:80
  65.7 12.2 %all-to-all-start.3 = ((s32[16,2,1]{1,2,0:T(1,128)}), s32[16,2,1]{1,2,0:T(1,128)S(1)}, u32[]{:S(2)}, u32[]{:S(2)}) async-start(s32[16,2,1]{1,2,0:T(1,128)} %all-to-all-done.2), calls=%async_computation.3 | async-start | bytes 16384 | tf_op jit(solution)/shard_map/all_to_all | solution.py:79
  113.1 13.1 %all-to-all-start = ((bf16[16,2,192]{2,1,0:T(2,128)(2,1)}), bf16[16,2,192]{2,1,0:T(2,128)(2,1)}, u32[]{:S(2)}, u32[]{:S(2)}) async-start(bf16[16,2,192]{2,1,0:T(2,128)(2,1)} %reshape.90), calls=%async_computation | async-start | bytes 32768 | tf_op jit(solution)/shard_map/all_to_all | solution.py:73
  126.2 11.9 %all-to-all-start.1 = ((bf16[16,2,192]{2,1,0:T(2,128)(2,1)}), bf16[16,2,192]{2,1,0:T(2,128)(2,1)S(1)}, u32[]{:S(2)}, u32[]{:S(2)}) async-start(bf16[16,2,192]{2,1,0:T(2,128)(2,1)} %all-to-all-done), calls=%async_computation.1 | async-start | bytes 32768 | tf_op jit(solution)/shard_map/all_to_all | solution.py:72
  138.8 45.7 %all-gather.6.cloned.1.call-start = ((), (), s32[]{:S(2)}) async-start(), calls=%async_computation.5 | async-start | bytes 3342336 | tf_op jit(solution)/shard_map/while/body/eval_jaxpr/all_gather | solution.py:11
  187.6 5.8 copy-start.2
  324.7 47.0 %all-gather.6.cloned.1.call-start = ((), (), s32[]{:S(2)}) async-start(), calls=%async_computation.5 | async-start | bytes 3342336 | tf_op jit(solution)/shard_map/while/body/eval_jaxpr/all_gather | solution.py:11
  374.8 5.8 copy-start.2
  511.9 46.3 %all-gather.6.cloned.1.call-start = ((), (), s32[]{:S(2)}) async-start(), calls=%async_computation.5 | async-start | bytes 3342336 | tf_op jit(solution)/shard_map/while/body/eval_jaxpr/all_gather | solution.py:11
  561.3 5.8 copy-start.2
  698.4 47.0 %all-gather.6.cloned.1.call-start = ((), (), s32[]{:S(2)}) async-start(), calls=%async_computation.5 | async-start | bytes 3342336 | tf_op jit(solution)/shard_map/while/body/eval_jaxpr/all_gather | solution.py:11
  748.5 5.8 copy-start.2
Sparse Core Ops, SparseCore 0:
  50.9 59.5 all-reduce.4
  141.8 42.7 all-gather.5
  327.6 44.0 all-gather.5
  515.7 42.5 all-gather.5
  701.2 44.1 all-gather.5
